TPU v7x, 32 devices: a whole 2x2x4 slice. The times are simulated.
32 devices in a mesh: row: 16 (over z, y, x), col: 2 (over core).
Axes of the slice: x: 2, y: 2, z: 4, core: 2. Of those that a mesh axis runs over, the one named last changes fastest.
Arguments:
- panel: bfloat16 [65536, 256], P('row'), may hold values from -400 to 400, as said below
- slab: bfloat16 [65536, 1024], P('row', 'col'), may hold values from -300 to 300
Outputs:
- factor: float32 [256, 256], P(None, 'col')
- coupling: float32 [256, 1024], P(None, 'col')
- remainder: bfloat16 [65536, 1024], P('row', 'col')
Inputs may be any that keep to these rules, and one draw needn't show every extreme that they name: panel has full column rank.
All inputs are finite; a program needn't handle non-finite values.
Results may differ from a plain program's by a relative error of at most 0.015.
The roundings to bfloat16 on the way count: a program that leaves them out, or rounds other values in their place, can miss the bound.
Values sent between devices are 32-bit elements; how exact they have to be, the bound alone decides.
A program may use at most 64 MiB of HBM per device.

v0:
```python
import jax
import jax.numpy as jnp
from jax import lax
from jax.sharding import PartitionSpec as P


def matmul(left, right):
    return jnp.dot(left, right, precision=lax.Precision.HIGHEST)


def factor_inverse(gram):
    order = gram.shape[0]
    if order == 1:
        root = jnp.sqrt(gram)
        return (root, 1.0 / root)
    half = order // 2
    upper_left, upper_inv = factor_inverse(gram[:half, :half])
    coupled = matmul(upper_inv.T, gram[:half, half:])
    lower_right, lower_inv = factor_inverse(gram[half:, half:] - matmul(coupled.T, coupled))
    zeros_block = jnp.zeros((order - half, half), gram.dtype)
    whole = jnp.concatenate(
        [
            jnp.concatenate([upper_left, coupled], axis=1),
            jnp.concatenate([zeros_block, lower_right], axis=1),
        ],
        axis=0,
    )
    corner = -matmul(matmul(upper_inv, coupled), lower_inv)
    inverse = jnp.concatenate(
        [
            jnp.concatenate([upper_inv, corner], axis=1),
            jnp.concatenate([zeros_block, lower_inv], axis=1),
        ],
        axis=0,
    )
    return (whole, inverse)


def upper_factor(gram):
    return factor_inverse(gram)[0]


def on_device(panel, slab):
    total_rows = panel.shape[0] * lax.axis_size("row")
    scale = 1.0 / total_rows
    contract = (((0,), (0,)), ((), ()))
    local_gram = lax.dot_general(panel, panel, contract, preferred_element_type=jnp.float32) * scale
    local_cross = lax.dot_general(panel, slab, contract, preferred_element_type=jnp.float32) * scale
    factor = upper_factor(lax.psum(local_gram, "row"))
    cross = lax.psum(local_cross, "row")
    inverse = factor_inverse(matmul(factor.T, factor))[1]
    coupling = matmul(inverse.T, cross)
    update = matmul(inverse, coupling).astype(jnp.bfloat16)
    remainder = (
        slab.astype(jnp.float32) - jnp.dot(panel, update, preferred_element_type=jnp.float32)
    ).astype(jnp.bfloat16)
    share = factor.shape[1] // lax.axis_size("col")
    factor_part = lax.dynamic_slice_in_dim(factor, lax.axis_index("col") * share, share, 1)
    return (factor_part, coupling, remainder)


def solution(mesh):
    return jax.shard_map(
        on_device,
        mesh=mesh,
        in_specs=(P("row", None), P("row", "col")),
        out_specs=(P(None, "col"), P(None, "col"), P("row", "col")),
        check_vma=False,
    )
```

profile of v0, /device:TPU:0, one launch (start us, length us, event | category | flops | bytes accessed | tf_op | source)
XLA Modules:
  0.0 1080.7 jit_solution(11859568985775000691)
XLA Ops:
  7.2 1.5 copy-done
  8.8 1.4 convolution_multiply_fusion.1
  10.2 0.8 copy-done.2
  11.0 2.1 convolution_multiply_fusion
  13.1 6.3 copy.270
  19.5 108.3 %all-reduce.377.cloned.1.call-done = (f32[256,256]{1,0:T(8,128)}, f32[256,512]{1,0:T(8,128)}) async-done(((f32[256,256]{1,0:T(8,128)}, f32[256,512]{1,0:T(8,128)}), (f32[256,256]{1,0:T(8,128)}, f32[256,512]{1,0:T(8,128)})) %all-reduce.377.cloned.1.call-update) | async-done | bytes 786448 | tf_op jit(solution)/shard_map/psum | solution.py:49
  127.8 1.5 fusion.2838
  131.4 0.8 fusion.2263
  132.4 0.9 convolution_subtract_fusion.253
  136.3 0.9 fusion.1810
  137.2 0.9 convolution_subtract_fusion.125
  144.9 1.0 fusion.1254
  145.9 0.9 convolution_subtract_fusion.61
  146.7 0.7 fusion.2900
  150.1 0.7 fusion.3090
  161.0 1.0 fusion.777
  162.0 0.9 convolution_subtract_fusion.29
  166.2 0.7 fusion.3088
  177.1 0.7 fusion.2899
  180.5 0.7 fusion.3086
  184.1 0.7 fusion.2961
  191.7 1.0 fusion.450
  192.7 0.9 convolution_subtract_fusion.13
  197.0 0.7 fusion.3084
  200.6 0.7 fusion.2960
  207.7 0.7 fusion.2898
  221.8 0.7 fusion.2867
  225.3 0.7 fusion.3080
  243.1 0.7 fusion.2957
  251.4 1.1 fusion.237
  252.5 1.0 convolution_subtract_fusion.5
  267.4 0.7 fusion.2896
  270.7 0.7 fusion.3074
  274.1 0.7 fusion.2955
  299.0 0.7 fusion.3070
  314.0 0.7 fusion.3068
  317.5 0.7 fusion.2952
  345.7 0.7 fusion.2950
  359.9 0.7 fusion.2949
  376.0 0.7 fusion.2948
  390.1 0.7 fusion.2947
  404.3 0.7 fusion.2946
  407.6 0.7 fusion.3055
  415.0 0.7 fusion.3054
  418.5 0.7 fusion.2945
  502.4 0.7 fusion.3042
  556.6 0.7 fusion.2886
  571.3 0.7 fusion.2861
  599.5 0.7 fusion.3029
  653.5 0.7 fusion.3022
  674.7 0.7 fusion.3019
  681.6 0.7 fusion.3018
  695.6 0.7 fusion.3016
  738.0 0.7 fusion.3010
  752.2 0.7 fusion.3008
  780.3 0.7 fusion.3004
  851.3 0.7 fusion.2994
  865.3 0.7 fusion.2992
  893.5 0.7 fusion.2988
  950.1 0.7 fusion.2980
  1061.5 0.7 fusion.2835
  1062.2 0.8 copy-done.5
  1063.7 3.3 fusion
  1067.0 6.4 copy.271
  (1854 shorter events, 380.2 us)
Async XLA Ops:
  7.2 1.6 copy-start
  7.2 120.6 %all-reduce.377.cloned.1.call-start = ((), (), s32[]{:S(2)}) async-start(), calls=%async_computation | async-start | bytes 1572864 | tf_op jit(solution)/shard_map/psum | solution.py:49
  8.8 2.3 copy-start.2
  127.8 240.6 %copy-start.3 = (f32[256,256]{1,0:T(8,128)S(1)}, f32[256,256]{1,0:T(8,128)}, u32[]{:S(2)}) copy-start(f32[256,256]{1,0:T(8,128)} %get-tuple-element.6) | copy-start | bytes 786436
  833.0 228.4 %copy-start.4 = (f32[256,512]{1,0:T(8,128)S(1)}, f32[256,512]{1,0:T(8,128)}, u32[]{:S(2)}) copy-start(f32[256,512]{1,0:T(8,128)} %get-tuple-element.7) | copy-start | bytes 1572868
  1059.8 3.9 copy-start.1
  1062.2 0.8 copy-start.5
Sparse Core Ops, SparseCore 0:
  14.0 113.7 all-reduce.376
where the time goes:
time: 1100 us; the launch traced here: 1080 us
  between operations  528 us (48%)
  matrix products  206 us (19%)
  local copies, waits for them, and re-layouts  198 us (18%)
  waiting for transfers between devices  108 us (10%)
  other arithmetic  40.6 us (4%)
    dot_general x1005, matrix products, matmul(): return jnp.dot(left, right, precision=lax.Precision.HIGHEST)  199 us
    slice x256, local copies, waits for them, and re-layouts, factor_inverse(): coupled = matmul(upper_inv.T, gram[:half, half:])  172 us
    psum x1, waiting for transfers between devices, on_device(): factor = upper_factor(lax.psum(local_gram, 'row'))  108 us
    concatenate x374, other arithmetic, factor_inverse(): jnp.concatenate([jnp.concatenate([upper_inv, corner], axis=1), jnp.concat...  30.4 us
  transfers between devices with their start and end apart: 1, of which 1 were waited for; matrix products, arithmetic and copies ran while one was open for 1% of the time, Pallas kernels for 0%

commit v1 on v0

v1 whole, which is shorter than its diff:
```python
import jax
import jax.numpy as jnp
from jax import lax
from jax.experimental import pallas as pl
from jax.experimental.pallas import tpu as pltpu

HI = lax.Precision.HIGHEST


def mm(a, b, ca=1, cb=0):
    return lax.dot_general(a, b, (((ca,), (cb,)), ((), ())), precision=HI, preferred_element_type=jnp.float32)


def eliminate(block, r_ref, w_ref):
    n = block.shape[0]
    groups = n // 8
    lane = lax.broadcasted_iota(jnp.int32, (8, n), 1)
    sub = lax.broadcasted_iota(jnp.int32, (8, n), 0)
    a = [block[8 * t : 8 * t + 8, :] for t in range(groups)]
    w = [jnp.where(lane == sub + 8 * t, 1.0, 0.0).astype(jnp.float32) for t in range(groups)]

    def group(g, carry):
        a, w = list(carry[0]), list(carry[1])
        for j in range(8):
            inv = lax.rsqrt(jnp.broadcast_to(a[0][j : j + 1, j : j + 1], (8, n)))
            arow = jnp.broadcast_to(a[0][j : j + 1, :], (8, n)) * inv
            wrow = jnp.broadcast_to(w[0][j : j + 1, :], (8, n)) * inv
            for t in range(groups):
                col = jnp.broadcast_to(a[t][:, j : j + 1], (8, n)) * inv
                if t == 0:
                    below = sub > j
                    here = sub == j
                    a[0], w[0] = (
                        jnp.where(here, arow, jnp.where(below, a[0] - col * arow, a[0])),
                        jnp.where(here, wrow, jnp.where(below, w[0] - col * wrow, w[0])),
                    )
                else:
                    a[t] = a[t] - col * arow
                    w[t] = w[t] - col * wrow
        start = pl.multiple_of(8 * g, 8)
        r = pltpu.roll(a[0], 8 * g, 1)
        r_ref[pl.ds(start, 8), :] = jnp.where(lane >= sub + 8 * g, r, 0.0)
        w_ref[pl.ds(start, 8), :] = w[0]
        zero = jnp.zeros((8, n), jnp.float32)
        a = [pltpu.roll(x, n - 8, 1) for x in a[1:]] + [zero]
        w = w[1:] + [zero]
        return tuple(a), tuple(w)

    lax.fori_loop(0, groups, group, (tuple(a), tuple(w)))


def factor_kernel(gram_ref, factor_ref, invt_ref, r_ref, w_ref):
    h = gram_ref.shape[0] // 2
    eliminate(gram_ref[:h, :h], r_ref, w_ref)
    w1 = w_ref[...]
    factor_ref[:h, :h] = r_ref[...]
    invt_ref[:h, :h] = w1
    r12 = mm(w1, gram_ref[:h, h:])
    factor_ref[:h, h:] = r12
    factor_ref[h:, :h] = jnp.zeros((h, h), jnp.float32)
    invt_ref[:h, h:] = jnp.zeros((h, h), jnp.float32)
    eliminate(gram_ref[h:, h:] - mm(r12, r12, 0, 0), r_ref, w_ref)
    w2 = w_ref[...]
    factor_ref[h:, h:] = r_ref[...]
    invt_ref[h:, h:] = w2
    invt_ref[h:, :h] = -mm(w2, mm(r12, w1, 0, 0))


def factor_and_invt(gram):
    n = gram.shape[0]
    h = n // 2
    out = jax.ShapeDtypeStruct((n, n), jnp.float32)
    return pl.pallas_call(
        factor_kernel,
        out_shape=(out, out),
        scratch_shapes=[pltpu.VMEM((h, h), jnp.float32), pltpu.VMEM((h, h), jnp.float32)],
        cost_estimate=pl.CostEstimate(flops=60_000_000, bytes_accessed=3 * n * n * 4, transcendentals=n),
        name="factor",
    )(gram)


def on_device(panel, slab):
    total_rows = panel.shape[0] * lax.axis_size("row")
    scale = 1.0 / total_rows
    contract = (((0,), (0,)), ((), ()))
    gram = lax.psum(lax.dot_general(panel, panel, contract, preferred_element_type=jnp.float32) * scale, "row")
    local_cross = lax.dot_general(panel, slab, contract, preferred_element_type=jnp.float32) * scale
    cross = lax.psum(local_cross, "row")
    factor, invt = factor_and_invt(gram)
    coupling = mm(invt, cross)
    update = mm(invt, coupling, 0, 0).astype(jnp.bfloat16)
    remainder = (slab.astype(jnp.float32) - jnp.dot(panel, update, preferred_element_type=jnp.float32)).astype(jnp.bfloat16)
    share = factor.shape[1] // lax.axis_size("col")
    factor_part = lax.dynamic_slice_in_dim(factor, lax.axis_index("col") * share, share, 1)
    return (factor_part, coupling, remainder)


def solution(mesh):
    from jax.sharding import PartitionSpec as P

    return jax.shard_map(
        on_device,
        mesh=mesh,
        in_specs=(P("row", None), P("row", "col")),
        out_specs=(P(None, "col"), P(None, "col"), P("row", "col")),
        check_vma=False,
    )
```

time: 1100 us -> 186 us (0.17); the launches traced: 1080 us -> 185 us
  between operations: 528 us -> 14.1 us
  matrix products: 206 us -> 12.4 us
  local copies, waits for them, and re-layouts: 198 us -> 15.8 us
  other arithmetic: 40.6 us -> 0 us
  Pallas kernels: 0 us -> 34.4 us
    dot_general x1005 -> x2, matrix products: 199 us -> 3.49 us  [mm(): lax.dot_general(a, b, (((ca,), (cb,)), ((), ())), precision=HI, preferred...]
    slice x263 -> x0, local copies, waits for them, and re-layouts: 172 us -> none  [the longest x256 172 us: factor_inverse(): coupled = matmul(upper_inv.T, gram[:half, half:])]
    concatenate x501 -> x0, other arithmetic: 40.6 us -> none  [the longest x374 30.4 us: factor_inverse(): jnp.concatenate([jnp.concatenate([upper_inv, corner], axis=1), jnp.concat...]
    pallas_call x0 -> x1, Pallas kernels: none -> 34.4 us  [factor_and_invt(): pl.pallas_call(factor_kernel, out_shape=(out, out), scratch_shapes=[pltpu...]
  transfers between devices with their start and end apart: 1 -> 1, of which waited for: 1 -> 1; matrix products, arithmetic and copies ran while one was open for 1% -> 3% of each run, Pallas kernels for 0% -> 0%
where the time goes in v1:
time: 186 us; the launch traced here: 185 us
  waiting for transfers between devices  108 us (58%)
  Pallas kernels  34.4 us (18%)
  local copies, waits for them, and re-layouts  15.8 us (8%)
  between operations  14.1 us (8%)
  matrix products  12.4 us (7%)
    psum x1, waiting for transfers between devices, on_device(): lax.psum(lax.dot_general(panel, panel, contract, preferred_element_type=j...  108 us
    pallas_call x1, Pallas kernels, factor_and_invt(): pl.pallas_call(factor_kernel, out_shape=(out, out), scratch_shapes=[pltpu...  34.4 us
    unnamed x10, local copies, waits for them, and re-layouts  15.2 us
    dot_general x1, matrix products, on_device(): jnp.dot(panel, update, preferred_element_type=jnp.float32)  5.44 us
  transfers between devices with their start and end apart: 1, of which 1 were waited for; matrix products, arithmetic and copies ran while one was open for 3% of the time, Pallas kernels for 0%

profile of v1, /device:TPU:0, one launch (start us, length us, event | category | flops | bytes accessed | tf_op | source)
XLA Modules:
  0.0 185.1 jit_solution(6760276120426760906)
XLA Ops:
  7.2 0.0 copy-start
  7.2 0.0 all-reduce.3.cloned.1.call-start
  7.2 1.5 copy-done
  8.8 0.0 copy-start.1
  8.8 1.4 convolution_multiply_fusion.1
  10.2 0.8 copy-done.1
  11.0 2.1 %convolution_multiply_fusion = f32[256,512]{1,0:T(8,128)} fusion(bf16[4096,256]{1,0:T(8,128)(2,1)S(1)} %copy-done, bf16[4096,512]{1,0:T(8,128)(2,1)S(1)} %copy-done.1), kind=kOutput, calls=%fused_computation.2 | convolution fusion | flops 1073872896 | bytes 6815744 | tf_op jit(solution)/shard_map/dot_general | solution.py:87
  13.1 0.0 all-reduce.3.cloned.1.call-update
  13.1 6.3 %copy.5 = bf16[4096,512]{0,1:T(8,128)(2,1)} copy(bf16[4096,512]{1,0:T(8,128)(2,1)} %param.3) | data formatting | bytes 8388608 | tf_op args[1]
  19.5 108.3 %all-reduce.3.cloned.1.call-done = (f32[256,256]{1,0:T(8,128)}, f32[256,512]{1,0:T(8,128)}) async-done(((f32[256,256]{1,0:T(8,128)}, f32[256,512]{1,0:T(8,128)}), (f32[256,256]{1,0:T(8,128)}, f32[256,512]{1,0:T(8,128)})) %all-reduce.3.cloned.1.call-update) | async-done | bytes 786448 | tf_op jit(solution)/shard_map/psum | solution.py:86
  127.8 34.4 %factor.1 = (f32[256,256]{1,0:T(8,128)}, f32[256,256]{1,0:T(8,128)}) custom-call(f32[256,256]{1,0:T(8,128)} %get-tuple-element.10.gram_ref), custom_call_target="tpu_custom_call" | custom-call | flops 60000000 | bytes 786432 | tf_op jit(solution)/shard_map/factor/pallas_call | solution.py:73
  162.1 1.7 fusion.1
  163.9 0.0 copy-start.2
  163.9 1.8 convolution_convert_fusion
  165.7 5.4 %fusion = bf16[4096,512]{0,1:T(8,128)(2,1)} fusion(bf16[4096,512]{0,1:T(8,128)(2,1)} %copy.5, bf16[256,512]{1,0:T(8,128)(2,1)S(1)} %convolution_convert_fusion, bf16[4096,256]{1,0:T(8,128)(2,1)S(1)} %copy-done), kind=kOutput, calls=%fused_computation.1 | convolution fusion | flops 1080033280 | bytes 10747904 | tf_op jit(solution)/shard_map/dot_general | solution.py:92
  171.1 0.0 copy-done.2
  171.1 0.0 copy-start.3
  171.1 6.4 %copy.6 = bf16[4096,512]{1,0:T(8,128)(2,1)} copy(bf16[4096,512]{0,1:T(8,128)(2,1)} %fusion) | data formatting | bytes 8388608
  177.6 0.0 copy-done.3
  177.6 0.7 constant_dynamic-slice_fusion
Async XLA Ops:
  7.2 1.6 copy-start
  7.2 120.6 %all-reduce.3.cloned.1.call-start = ((), (), s32[]{:S(2)}) async-start(), calls=%async_computation | async-start | bytes 1572864 | tf_op jit(solution)/shard_map/psum | solution.py:86
  8.8 2.3 %copy-start.1 = (bf16[4096,512]{1,0:T(8,128)(2,1)S(1)}, bf16[4096,512]{1,0:T(8,128)(2,1)}, u32[]{:S(2)}) copy-start(bf16[4096,512]{1,0:T(8,128)(2,1)} %param.3) | copy-start | bytes 12582916
  163.9 7.2 %copy-start.2 = (f32[256,512]{1,0:T(8,128)}, f32[256,512]{1,0:T(8,128)S(1)}, u32[]{:S(2)}) copy-start(f32[256,512]{1,0:T(8,128)S(1)} %fusion.1) | copy-start | bytes 1572868
  171.1 6.4 %copy-start.3 = (f32[256,256]{1,0:T(8,128)S(1)}, f32[256,256]{1,0:T(8,128)}, u32[]{:S(2)}) copy-start(f32[256,256]{1,0:T(8,128)} %get-tuple-element.5) | copy-start | bytes 786436
Sparse Core Ops, SparseCore 0:
  14.0 113.7 all-reduce.2

commit v2 on v1

--- a/solution.py
+++ b/solution.py
@@ -1,8 +1,11 @@
+import functools
+
 import jax
 import jax.numpy as jnp
 from jax import lax
 from jax.experimental import pallas as pl
 from jax.experimental.pallas import tpu as pltpu
+from jax.sharding import PartitionSpec as P
 
 HI = lax.Precision.HIGHEST
 
@@ -49,55 +52,244 @@
     lax.fori_loop(0, groups, group, (tuple(a), tuple(w)))
 
 
-def factor_kernel(gram_ref, factor_ref, invt_ref, r_ref, w_ref):
-    h = gram_ref.shape[0] // 2
-    eliminate(gram_ref[:h, :h], r_ref, w_ref)
+def fused_kernel(
+    n, ncol, gram_ref, cross_ref, factor_ref, invt_ref, full_ref,
+    gbuf, cbuf, gfull, cfull, gown, cown, r_ref, w_ref,
+    gs_send, gs_recv, ga_send, ga_recv, fw_send, fw_recv, cs_send, cs_recv, ca_send, ca_recv,
+):
+    me, mc = lax.axis_index("row"), lax.axis_index("col")
+    order = gram_ref.shape[1]
+    part = gram_ref.shape[0]
+    gchunk, cchunk = gown.shape[0], cown.shape[0]
+    gowners, cowners = part // gchunk, order // cchunk
+
+    def peers(body):
+        def step(k, _):
+            body(lax.rem(me + k, n))
+            return 0
+
+        lax.fori_loop(1, n, step, 0)
+
+    def cols(body):
+        def step(k, _):
+            body(lax.rem(mc + k, ncol))
+            return 0
+
+        lax.fori_loop(1, ncol, step, 0)
+
+    def owned(owners, who, body):
+        if owners == n:
+            body()
+        else:
+            pl.when(who < owners)(body)
+
+    def remote(src, dst, send, recv, row, col):
+        return pltpu.make_async_remote_copy(
+            src_ref=src, dst_ref=dst, send_sem=send, recv_sem=recv,
+            device_id={"row": row, "col": col}, device_id_type=pl.DeviceIdType.MESH,
+        )
+
+    barrier = pltpu.get_barrier_semaphore()
+    peers(lambda p: pl.semaphore_signal(barrier, inc=1, device_id={"row": p, "col": mc}, device_id_type=pl.DeviceIdType.MESH))
+    cols(lambda q: pl.semaphore_signal(barrier, inc=1, device_id={"row": me, "col": q}, device_id_type=pl.DeviceIdType.MESH))
+    pl.semaphore_wait(barrier, n + ncol - 2)
+
+    def rows(owner, chunk):
+        return pl.ds(pl.multiple_of(owner * chunk, 8), chunk)
+
+    def grows(owner, col):
+        return pl.ds(pl.multiple_of(col * part + owner * gchunk, 8), gchunk)
+
+    def gs(src, dst):
+        return remote(gram_ref.at[rows(dst, gchunk)], gbuf.at[src], gs_send.at[dst], gs_recv.at[src], dst, mc)
+
+    def ga(owner, dst):
+        return remote(gown, gfull.at[grows(owner, mc)], ga_send.at[dst], ga_recv.at[owner], dst, mc)
+
+    def fw(owner, col, dst):
+        return remote(
+            gfull.at[grows(owner, col)], gfull.at[grows(owner, col)],
+            fw_send.at[owner, dst], fw_recv.at[owner, col], me, dst,
+        )
+
+    def cs(src, dst):
+        return remote(cross_ref.at[rows(dst, cchunk)], cbuf.at[src], cs_send.at[dst], cs_recv.at[src], dst, mc)
+
+    def ca(owner, dst):
+        return remote(cown, cfull.at[rows(owner, cchunk)], ca_send.at[dst], ca_recv.at[owner], dst, mc)
+
+    peers(lambda p: owned(gowners, p, lambda: gs(me, p).start()))
+
+    def sum_gram():
+        gown[...] = gram_ref[rows(me, gchunk), :]
+
+        def add(p):
+            gs(p, me).wait_recv()
+            gown[...] += gbuf[p]
+
+        peers(add)
+        gfull[grows(me, mc), :] = gown[...]
+        peers(lambda p: ga(me, p).start())
+        cols(lambda q: remote(
+            gown, gfull.at[grows(me, mc)], fw_send.at[me, q], fw_recv.at[me, mc], me, q).start())
+
+    owned(gowners, me, sum_gram)
+    peers(lambda p: owned(cowners, p, lambda: cs(me, p).start()))
+
+    def relay(p):
+        def go():
+            ga(p, me).wait_recv()
+            cols(lambda q: fw(p, mc, q).start())
+
+        owned(gowners, p, go)
+
+    peers(relay)
+
+    def relayed(q):
+        def each(o, _):
+            fw(o, q, mc).wait_recv()
+            return 0
+
+        lax.fori_loop(0, gowners, each, 0)
+
+    cols(relayed)
+
+    h = order // 2
+    eliminate(gfull[:h, :h], r_ref, w_ref)
     w1 = w_ref[...]
     factor_ref[:h, :h] = r_ref[...]
     invt_ref[:h, :h] = w1
-    r12 = mm(w1, gram_ref[:h, h:])
+    r12 = mm(w1, gfull[:h, h:])
     factor_ref[:h, h:] = r12
     factor_ref[h:, :h] = jnp.zeros((h, h), jnp.float32)
     invt_ref[:h, h:] = jnp.zeros((h, h), jnp.float32)
-    eliminate(gram_ref[h:, h:] - mm(r12, r12, 0, 0), r_ref, w_ref)
+    lower = gfull[h:, h:] - mm(r12, r12, 0, 0)
+
+    def sum_cross():
+        cown[...] = cross_ref[rows(me, cchunk), :]
+
+        def add(p):
+            cs(p, me).wait_recv()
+            cown[...] += cbuf[p]
+
+        peers(add)
+        cfull[rows(me, cchunk), :] = cown[...]
+        peers(lambda p: ca(me, p).start())
+
+    owned(cowners, me, sum_cross)
+
+    eliminate(lower, r_ref, w_ref)
     w2 = w_ref[...]
     factor_ref[h:, h:] = r_ref[...]
     invt_ref[h:, h:] = w2
     invt_ref[h:, :h] = -mm(w2, mm(r12, w1, 0, 0))
 
-
-def factor_and_invt(gram):
-    n = gram.shape[0]
-    h = n // 2
-    out = jax.ShapeDtypeStruct((n, n), jnp.float32)
+    peers(lambda p: owned(cowners, p, lambda: ca(p, me).wait_recv()))
+    full_ref[...] = cfull[...]
+    peers(lambda p: owned(gowners, p, lambda: gs(me, p).wait_send()))
+    peers(lambda p: owned(cowners, p, lambda: cs(me, p).wait_send()))
+    owned(gowners, me, lambda: peers(lambda p: ga(me, p).wait_send()))
+    owned(cowners, me, lambda: peers(lambda p: ca(me, p).wait_send()))
+
+    def sent(q):
+        def each(o, _):
+            fw(o, mc, q).wait_send()
+            return 0
+
+        lax.fori_loop(0, gowners, each, 0)
+
+    cols(sent)
+
+
+def sums_and_factor(gram, cross, n, ncol):
+    part, order = gram.shape
+    width = cross.shape[1]
+    gchunk = max(8, part // n)
+    cchunk = max(8, order // n)
+    f32 = jnp.float32
+    dma = pltpu.SemaphoreType.DMA
+    square = jax.ShapeDtypeStruct((order, order), f32)
+    h = order // 2
     return pl.pallas_call(
-        factor_kernel,
-        out_shape=(out, out),
-        scratch_shapes=[pltpu.VMEM((h, h), jnp.float32), pltpu.VMEM((h, h), jnp.float32)],
-        cost_estimate=pl.CostEstimate(flops=60_000_000, bytes_accessed=3 * n * n * 4, transcendentals=n),
-        name="factor",
-    )(gram)
+        functools.partial(fused_kernel, n, ncol),
+        out_shape=(square, square, jax.ShapeDtypeStruct((order, width), f32)),
+        in_specs=[pl.BlockSpec(memory_space=pltpu.VMEM)] * 2,
+        out_specs=[pl.BlockSpec(memory_space=pltpu.VMEM)] * 3,
+        scratch_shapes=[
+            pltpu.VMEM((n, gchunk, order), f32),
+            pltpu.VMEM((n, cchunk, width), f32),
+            pltpu.VMEM((order, order), f32),
+            pltpu.VMEM((order, width), f32),
+            pltpu.VMEM((gchunk, order), f32),
+            pltpu.VMEM((cchunk, width), f32),
+            pltpu.VMEM((h, h), f32),
+            pltpu.VMEM((h, h), f32),
+            dma((n,)), dma((n,)), dma((n,)), dma((n,)),
+            dma((n, ncol)), dma((n, ncol)),
+            dma((n,)), dma((n,)), dma((n,)), dma((n,)),
+        ],
+        compiler_params=pltpu.CompilerParams(collective_id=0, has_side_effects=True),
+        name="sums_and_factor",
+    )(gram, cross)
+
+
+def finish_kernel(factor_ref, invt_ref, cross_ref, panel_ref, slab_ref, part_ref, coupling_ref, out_ref, update):
+    @pl.when(pl.program_id(0) == 0)
+    def _():
+        share = part_ref.shape[1]
+        for q in range(factor_ref.shape[1] // share):
+
+            @pl.when(lax.axis_index("col") == q)
+            def _(q=q):
+                part_ref[...] = factor_ref[:, q * share : (q + 1) * share]
+
+        invt = invt_ref[...]
+        coupling = mm(invt, cross_ref[...])
+        coupling_ref[...] = coupling
+        update[...] = mm(invt, coupling, 0, 0).astype(jnp.bfloat16)
+
+    product = jnp.dot(panel_ref[...], update[...], preferred_element_type=jnp.float32)
+    out_ref[...] = (slab_ref[...].astype(jnp.float32) - product).astype(jnp.bfloat16)
+
+
+def finish(factor, invt, cross, panel, slab, ncol):
+    order, width = cross.shape
+    height = panel.shape[0]
+    tile = max(height // 8, 8)
+    share = order // ncol
+    whole = lambda shape: pl.BlockSpec(shape, lambda i: (0, 0))
+    return pl.pallas_call(
+        finish_kernel,
+        grid=(height // tile,),
+        out_shape=(
+            jax.ShapeDtypeStruct((order, share), jnp.float32),
+            jax.ShapeDtypeStruct((order, width), jnp.float32),
+            jax.ShapeDtypeStruct((height, width), jnp.bfloat16),
+        ),
+        in_specs=[
+            whole((order, order)), whole((order, order)), whole((order, width)),
+            pl.BlockSpec((tile, order), lambda i: (i, 0)),
+            pl.BlockSpec((tile, width), lambda i: (i, 0)),
+        ],
+        out_specs=(whole((order, share)), whole((order, width)), pl.BlockSpec((tile, width), lambda i: (i, 0))),
+        scratch_shapes=[pltpu.VMEM((order, width), jnp.bfloat16)],
+        name="finish",
+    )(factor, invt, cross, panel, slab)
 
 
 def on_device(panel, slab):
-    total_rows = panel.shape[0] * lax.axis_size("row")
-    scale = 1.0 / total_rows
+    n, ncol = lax.axis_size("row"), lax.axis_size("col")
+    scale = 1.0 / (panel.shape[0] * n)
     contract = (((0,), (0,)), ((), ()))
-    gram = lax.psum(lax.dot_general(panel, panel, contract, preferred_element_type=jnp.float32) * scale, "row")
-    local_cross = lax.dot_general(panel, slab, contract, preferred_element_type=jnp.float32) * scale
-    cross = lax.psum(local_cross, "row")
-    factor, invt = factor_and_invt(gram)
-    coupling = mm(invt, cross)
-    update = mm(invt, coupling, 0, 0).astype(jnp.bfloat16)
-    remainder = (slab.astype(jnp.float32) - jnp.dot(panel, update, preferred_element_type=jnp.float32)).astype(jnp.bfloat16)
-    share = factor.shape[1] // lax.axis_size("col")
-    factor_part = lax.dynamic_slice_in_dim(factor, lax.axis_index("col") * share, share, 1)
-    return (factor_part, coupling, remainder)
+    part = panel.shape[1] // ncol
+    mine = lax.dynamic_slice_in_dim(panel, lax.axis_index("col") * part, part, 1)
+    gram = lax.dot_general(mine, panel, contract, preferred_element_type=jnp.float32) * scale
+    cross = lax.dot_general(panel, slab, contract, preferred_element_type=jnp.float32) * scale
+    factor, invt, cross = sums_and_factor(gram, cross, n, ncol)
+    return finish(factor, invt, cross, panel, slab, ncol)
 
 
 def solution(mesh):
-    from jax.sharding import PartitionSpec as P
-
     return jax.shard_map(
         on_device,
         mesh=mesh,

time: 186 us -> 75.8 us (0.41)
  the two profiles are of different devices: /device:TPU:0 before, /device:TPU:9 now
where the time goes in v2:
time: 75.8 us; the launch traced here: 75.5 us
  Pallas kernels  67.3 us (89%)
  matrix products  7.47 us (10%)
    pallas_call x1, Pallas kernels, sums_and_factor(): pl.pallas_call(functools.partial(fused_kernel, n, ncol), out_shape=(squar...  57.8 us
    pallas_call x1, Pallas kernels, finish(): pl.pallas_call(finish_kernel, grid=(height // tile,), out_shape=(jax.Shap...  9.53 us
    dot_general x1, matrix products, on_device(): lax.dot_general(panel, slab, contract, preferred_element_type=jnp.float32)  4.25 us
    dot_general x1, matrix products, on_device(): lax.dot_general(mine, panel, contract, preferred_element_type=jnp.float32)  3.23 us

profile of v2, /device:TPU:9, one launch (start us, length us, event | category | flops | bytes accessed | tf_op | source)
XLA Modules:
  0.0 75.5 jit_solution(3342493778310634109)
XLA Ops:
  0.6 0.0 copy-start
  0.6 3.2 %convolution_multiply_fusion.1.gram_ref = f32[128,256]{1,0:T(8,128)} fusion(bf16[4096,256]{1,0:T(8,128)(2,1)} %panel_ref.1, s32[]{:T(128)S(6)} %select_n.3), kind=kOutput, calls=%fused_computation.1 | convolution fusion | flops 268468224 | bytes 3276804 | tf_op jit(solution)/shard_map/dot_general | solution.py:286
  3.9 0.0 copy-done
  3.9 4.2 %convolution_multiply_fusion.cross_ref = f32[256,512]{1,0:T(8,128)} fusion(bf16[4096,256]{1,0:T(8,128)(2,1)S(1)} %copy-done, bf16[4096,512]{1,0:T(8,128)(2,1)} %slab_ref.1), kind=kOutput, calls=%fused_computation | convolution fusion | flops 1073872896 | bytes 6815744 | tf_op jit(solution)/shard_map/dot_general | solution.py:287
  8.1 57.8 %sums_and_factor.1 = (f32[256,256]{1,0:T(8,128)}, f32[256,256]{1,0:T(8,128)}, f32[256,512]{1,0:T(8,128)}) custom-call(f32[128,256]{1,0:T(8,128)} %convolution_multiply_fusion.1.gram_ref, f32[256,512]{1,0:T(8,128)} %convolution_multiply_fusion.cross_ref), custom_call_target="tpu_custom_call" | custom-call | tf_op jit(solution)/shard_map/sums_and_factor/pallas_call | solution.py:213
  65.9 9.5 %finish.1 = (f32[256,128]{1,0:T(8,128)}, f32[256,512]{1,0:T(8,128)}, bf16[4096,512]{1,0:T(8,128)(2,1)}) custom-call(f32[256,256]{1,0:T(8,128)} %get-tuple-element.6.factor_ref, f32[256,256]{1,0:T(8,128)} %get-tuple-element.7.invt_ref, f32[256,512]{1,0:T(8,128)} %get-tuple-element.8.cross_ref, bf16[4096,256]{1,0:T(8,128)(2,1)} %panel_ref.1, ...), custom_call_target="tpu_custom_call" | custom-call | tf_op jit(solution)/shard_map/finish/pallas_call | solution.py:261
Async XLA Ops:
  0.6 3.2 %copy-start = (bf16[4096,256]{1,0:T(8,128)(2,1)S(1)}, bf16[4096,256]{1,0:T(8,128)(2,1)}, u32[]{:S(2)}) copy-start(bf16[4096,256]{1,0:T(8,128)(2,1)} %panel_ref.1) | copy-start | bytes 6291460

commit v3 on v2

--- a/solution.py
+++ b/solution.py
@@ -24,40 +24,40 @@
 
     def group(g, carry):
         a, w = list(carry[0]), list(carry[1])
+        top, wtop = a[0], w[0]
+        cols = [jnp.broadcast_to(top[:, j : j + 1], (8, n)) for j in range(8)]
+        scale = jnp.zeros((8, n), jnp.float32)
         for j in range(8):
-            inv = lax.rsqrt(jnp.broadcast_to(a[0][j : j + 1, j : j + 1], (8, n)))
-            arow = jnp.broadcast_to(a[0][j : j + 1, :], (8, n)) * inv
-            wrow = jnp.broadcast_to(w[0][j : j + 1, :], (8, n)) * inv
-            for t in range(groups):
-                col = jnp.broadcast_to(a[t][:, j : j + 1], (8, n)) * inv
-                if t == 0:
-                    below = sub > j
-                    here = sub == j
-                    a[0], w[0] = (
-                        jnp.where(here, arow, jnp.where(below, a[0] - col * arow, a[0])),
-                        jnp.where(here, wrow, jnp.where(below, w[0] - col * wrow, w[0])),
-                    )
-                else:
-                    a[t] = a[t] - col * arow
-                    w[t] = w[t] - col * wrow
+            inv = lax.rsqrt(jnp.broadcast_to(cols[j][j : j + 1, :], (8, n)))
+            scale = jnp.where(sub == j, inv, scale)
+            m = jnp.where(sub > j, cols[j], 0.0) * inv * inv
+            for i in range(j + 1, 8):
+                cols[i] = cols[i] - m * jnp.broadcast_to(cols[i][j : j + 1, :], (8, n))
+            top = top - m * jnp.broadcast_to(top[j : j + 1, :], (8, n))
+            wtop = wtop - m * jnp.broadcast_to(wtop[j : j + 1, :], (8, n))
+        top, wtop = top * scale, wtop * scale
         start = pl.multiple_of(8 * g, 8)
-        r = pltpu.roll(a[0], 8 * g, 1)
-        r_ref[pl.ds(start, 8), :] = jnp.where(lane >= sub + 8 * g, r, 0.0)
-        w_ref[pl.ds(start, 8), :] = w[0]
+        r_ref[pl.ds(start, 8), :] = jnp.where(lane >= sub + 8 * g, pltpu.roll(top, 8 * g, 1), 0.0)
+        w_ref[pl.ds(start, 8), :] = wtop
+        u = mm(top, jnp.concatenate([top, wtop], axis=1), 0, 0)
         zero = jnp.zeros((8, n), jnp.float32)
-        a = [pltpu.roll(x, n - 8, 1) for x in a[1:]] + [zero]
-        w = w[1:] + [zero]
+        a = [pltpu.roll(a[t] - u[8 * t : 8 * t + 8, :n], n - 8, 1) for t in range(1, groups)] + [zero]
+        w = [w[t] - u[8 * t : 8 * t + 8, n:] for t in range(1, groups)] + [zero]
         return tuple(a), tuple(w)
 
     lax.fori_loop(0, groups, group, (tuple(a), tuple(w)))
 
 
 def fused_kernel(
-    n, ncol, gram_ref, cross_ref, factor_ref, invt_ref, full_ref,
-    gbuf, cbuf, gfull, cfull, gown, cown, r_ref, w_ref,
+    n, ncol, scale, panel_hbm, slab_hbm, factor_ref, invt_ref, full_ref,
+    panel_ref, slab_ref, panel_sem, slab_sem, gram_ref, cross_ref, gbuf, cbuf, gfull, cfull, gown, cown, r_ref, w_ref,
     gs_send, gs_recv, ga_send, ga_recv, fw_send, fw_recv, cs_send, cs_recv, ca_send, ca_recv,
 ):
     me, mc = lax.axis_index("row"), lax.axis_index("col")
+    get_panel = pltpu.make_async_copy(panel_hbm, panel_ref, panel_sem)
+    get_panel.start()
+    get_slab = pltpu.make_async_copy(slab_hbm, slab_ref, slab_sem)
+    get_slab.start()
     order = gram_ref.shape[1]
     part = gram_ref.shape[0]
     gchunk, cchunk = gown.shape[0], cown.shape[0]
@@ -66,6 +66,13 @@
     def peers(body):
         def step(k, _):
             body(lax.rem(me + k, n))
+            return 0
+
+        lax.fori_loop(1, n, step, 0)
+
+    def sources(body):
+        def step(k, _):
+            body(lax.rem(me + n - k, n))
             return 0
 
         lax.fori_loop(1, n, step, 0)
@@ -92,6 +99,26 @@
     barrier = pltpu.get_barrier_semaphore()
     peers(lambda p: pl.semaphore_signal(barrier, inc=1, device_id={"row": p, "col": mc}, device_id_type=pl.DeviceIdType.MESH))
     cols(lambda q: pl.semaphore_signal(barrier, inc=1, device_id={"row": me, "col": q}, device_id_type=pl.DeviceIdType.MESH))
+    height = panel_ref.shape[0]
+    tile = height // 4
+    contract = (((0,), (0,)), ((), ()))
+    get_panel.wait()
+    for q in range(ncol):
+
+        @pl.when(mc == q)
+        def _(q=q):
+            gram_ref[...] = jnp.zeros_like(gram_ref)
+
+            def gram_step(t, _):
+                at = pl.ds(pl.multiple_of(t * tile, tile), tile)
+                gram_ref[...] += lax.dot_general(
+                    panel_ref[at, q * part : (q + 1) * part], panel_ref[at, :], contract, preferred_element_type=jnp.float32
+                )
+                return 0
+
+            lax.fori_loop(0, height // tile, gram_step, 0)
+
+    gram_ref[...] *= scale
     pl.semaphore_wait(barrier, n + ncol - 2)
 
     def rows(owner, chunk):
@@ -120,6 +147,17 @@
 
     peers(lambda p: owned(gowners, p, lambda: gs(me, p).start()))
 
+    get_slab.wait()
+    cross_ref[...] = jnp.zeros_like(cross_ref)
+
+    def cross_step(t, _):
+        at = pl.ds(pl.multiple_of(t * tile, tile), tile)
+        cross_ref[...] += lax.dot_general(panel_ref[at, :], slab_ref[at, :], contract, preferred_element_type=jnp.float32)
+        return 0
+
+    lax.fori_loop(0, height // tile, cross_step, 0)
+    cross_ref[...] *= scale
+
     def sum_gram():
         gown[...] = gram_ref[rows(me, gchunk), :]
 
@@ -127,7 +165,7 @@
             gs(p, me).wait_recv()
             gown[...] += gbuf[p]
 
-        peers(add)
+        sources(add)
         gfull[grows(me, mc), :] = gown[...]
         peers(lambda p: ga(me, p).start())
         cols(lambda q: remote(
@@ -143,7 +181,7 @@
 
         owned(gowners, p, go)
 
-    peers(relay)
+    sources(relay)
 
     def relayed(q):
         def each(o, _):
@@ -172,7 +210,7 @@
             cs(p, me).wait_recv()
             cown[...] += cbuf[p]
 
-        peers(add)
+        sources(add)
         cfull[rows(me, cchunk), :] = cown[...]
         peers(lambda p: ca(me, p).start())
 
@@ -201,9 +239,11 @@
     cols(sent)
 
 
-def sums_and_factor(gram, cross, n, ncol):
-    part, order = gram.shape
-    width = cross.shape[1]
+def sums_and_factor(panel, slab, n, ncol):
+    height, order = panel.shape
+    width = slab.shape[1]
+    part = order // ncol
+    scale = 1.0 / (height * n)
     gchunk = max(8, part // n)
     cchunk = max(8, order // n)
     f32 = jnp.float32
@@ -211,11 +251,16 @@
     square = jax.ShapeDtypeStruct((order, order), f32)
     h = order // 2
     return pl.pallas_call(
-        functools.partial(fused_kernel, n, ncol),
+        functools.partial(fused_kernel, n, ncol, scale),
         out_shape=(square, square, jax.ShapeDtypeStruct((order, width), f32)),
-        in_specs=[pl.BlockSpec(memory_space=pltpu.VMEM)] * 2,
+        in_specs=[pl.BlockSpec(memory_space=pl.ANY)] * 2,
         out_specs=[pl.BlockSpec(memory_space=pltpu.VMEM)] * 3,
         scratch_shapes=[
+            pltpu.VMEM(panel.shape, panel.dtype),
+            pltpu.VMEM(slab.shape, slab.dtype),
+            dma, dma,
+            pltpu.VMEM((part, order), f32),
+            pltpu.VMEM((order, width), f32),
             pltpu.VMEM((n, gchunk, order), f32),
             pltpu.VMEM((n, cchunk, width), f32),
             pltpu.VMEM((order, order), f32),
@@ -230,62 +275,73 @@
         ],
         compiler_params=pltpu.CompilerParams(collective_id=0, has_side_effects=True),
         name="sums_and_factor",
-    )(gram, cross)
-
-
-def finish_kernel(factor_ref, invt_ref, cross_ref, panel_ref, slab_ref, part_ref, coupling_ref, out_ref, update):
-    @pl.when(pl.program_id(0) == 0)
-    def _():
-        share = part_ref.shape[1]
-        for q in range(factor_ref.shape[1] // share):
-
-            @pl.when(lax.axis_index("col") == q)
-            def _(q=q):
-                part_ref[...] = factor_ref[:, q * share : (q + 1) * share]
-
-        invt = invt_ref[...]
-        coupling = mm(invt, cross_ref[...])
-        coupling_ref[...] = coupling
-        update[...] = mm(invt, coupling, 0, 0).astype(jnp.bfloat16)
-
-    product = jnp.dot(panel_ref[...], update[...], preferred_element_type=jnp.float32)
-    out_ref[...] = (slab_ref[...].astype(jnp.float32) - product).astype(jnp.bfloat16)
+    )(panel, slab)
+
+
+def finish_kernel(
+    tiles, factor_ref, invt_ref, cross_ref, panel_hbm, slab_hbm, part_ref, coupling_hbm, out_hbm,
+    panel_ref, slab_ref, out_ref, coupling_ref, panel_sem, slab_sem, out_sem, coupling_sem,
+):
+    tile = panel_ref.shape[0] // tiles
+    rows = [pl.ds(t * tile, tile) for t in range(tiles)]
+    get_panel = [pltpu.make_async_copy(panel_hbm.at[rows[t]], panel_ref.at[rows[t]], panel_sem.at[t]) for t in range(tiles)]
+    get_slab = [pltpu.make_async_copy(slab_hbm.at[rows[t]], slab_ref.at[rows[t]], slab_sem.at[t]) for t in range(tiles)]
+    put_out = [pltpu.make_async_copy(out_ref.at[rows[t]], out_hbm.at[rows[t]], out_sem.at[t]) for t in range(tiles)]
+    put_coupling = pltpu.make_async_copy(coupling_ref, coupling_hbm, coupling_sem)
+    for t in range(tiles):
+        get_panel[t].start()
+        get_slab[t].start()
+    share = part_ref.shape[1]
+    for q in range(factor_ref.shape[1] // share):
+
+        @pl.when(lax.axis_index("col") == q)
+        def _(q=q):
+            part_ref[...] = factor_ref[:, q * share : (q + 1) * share]
+
+    invt = invt_ref[...]
+    coupling = mm(invt, cross_ref[...])
+    coupling_ref[...] = coupling
+    put_coupling.start()
+    update = mm(invt, coupling, 0, 0).astype(jnp.bfloat16)
+    for t in range(tiles):
+        get_panel[t].wait()
+        get_slab[t].wait()
+        product = jnp.dot(panel_ref[rows[t], :], update, preferred_element_type=jnp.float32)
+        out_ref[rows[t], :] = (slab_ref[rows[t], :].astype(jnp.float32) - product).astype(jnp.bfloat16)
+        put_out[t].start()
+    for t in range(tiles):
+        put_out[t].wait()
+    put_coupling.wait()
 
 
 def finish(factor, invt, cross, panel, slab, ncol):
     order, width = cross.shape
-    height = panel.shape[0]
-    tile = max(height // 8, 8)
-    share = order // ncol
-    whole = lambda shape: pl.BlockSpec(shape, lambda i: (0, 0))
+    tiles = 8
+    vmem, hbm = pl.BlockSpec(memory_space=pltpu.VMEM), pl.BlockSpec(memory_space=pl.ANY)
+    dma = pltpu.SemaphoreType.DMA
     return pl.pallas_call(
-        finish_kernel,
-        grid=(height // tile,),
+        functools.partial(finish_kernel, tiles),
         out_shape=(
-            jax.ShapeDtypeStruct((order, share), jnp.float32),
+            jax.ShapeDtypeStruct((order, order // ncol), jnp.float32),
             jax.ShapeDtypeStruct((order, width), jnp.float32),
-            jax.ShapeDtypeStruct((height, width), jnp.bfloat16),
+            jax.ShapeDtypeStruct(slab.shape, slab.dtype),
         ),
-        in_specs=[
-            whole((order, order)), whole((order, order)), whole((order, width)),
-            pl.BlockSpec((tile, order), lambda i: (i, 0)),
-            pl.BlockSpec((tile, width), lambda i: (i, 0)),
+        in_specs=[vmem, vmem, vmem, hbm, hbm],
+        out_specs=(vmem, hbm, hbm),
+        scratch_shapes=[
+            pltpu.VMEM(panel.shape, panel.dtype),
+            pltpu.VMEM(slab.shape, slab.dtype),
+            pltpu.VMEM(slab.shape, slab.dtype),
+            pltpu.VMEM((order, width), jnp.float32),
+            dma((tiles,)), dma((tiles,)), dma((tiles,)), dma,
         ],
-        out_specs=(whole((order, share)), whole((order, width)), pl.BlockSpec((tile, width), lambda i: (i, 0))),
-        scratch_shapes=[pltpu.VMEM((order, width), jnp.bfloat16)],
         name="finish",
     )(factor, invt, cross, panel, slab)
 
 
 def on_device(panel, slab):
     n, ncol = lax.axis_size("row"), lax.axis_size("col")
-    scale = 1.0 / (panel.shape[0] * n)
-    contract = (((0,), (0,)), ((), ()))
-    part = panel.shape[1] // ncol
-    mine = lax.dynamic_slice_in_dim(panel, lax.axis_index("col") * part, part, 1)
-    gram = lax.dot_general(mine, panel, contract, preferred_element_type=jnp.float32) * scale
-    cross = lax.dot_general(panel, slab, contract, preferred_element_type=jnp.float32) * scale
-    factor, invt, cross = sums_and_factor(gram, cross, n, ncol)
+    factor, invt, cross = sums_and_factor(panel, slab, n, ncol)
     return finish(factor, invt, cross, panel, slab, ncol)
 
 

time: 75.8 us -> 53.1 us (0.70)
  the two profiles are of different devices: /device:TPU:9 before, /device:TPU:29 now
where the time goes in v3:
time: 53.1 us; the launch traced here: 52.9 us
  Pallas kernels  52.3 us (98%)
  between operations  0.64 us (1%)
    pallas_call x1, Pallas kernels, sums_and_factor(): pl.pallas_call(functools.partial(fused_kernel, n, ncol, scale), out_shape...  45.2 us
    pallas_call x1, Pallas kernels, finish(): pl.pallas_call(functools.partial(finish_kernel, tiles), out_shape=(jax.Sh...  7.08 us

profile of v3, /device:TPU:29, one launch (start us, length us, event | category | flops | bytes accessed | tf_op | source)
XLA Modules:
  0.0 52.9 jit_solution(16175602892935906105)
XLA Ops:
  0.6 45.2 %sums_and_factor.1 = (f32[256,256]{1,0:T(8,128)}, f32[256,256]{1,0:T(8,128)}, f32[256,512]{1,0:T(8,128)}) custom-call(bf16[4096,256]{1,0:T(8,128)(2,1)} %panel_hbm.3, bf16[4096,512]{1,0:T(8,128)(2,1)} %slab_hbm.3), custom_call_target="tpu_custom_call" | custom-call | tf_op jit(solution)/shard_map/sums_and_factor/pallas_call | solution.py:253
  45.8 7.1 %finish.1 = (f32[256,128]{1,0:T(8,128)}, f32[256,512]{1,0:T(8,128)}, bf16[4096,512]{1,0:T(8,128)(2,1)}) custom-call(f32[256,256]{1,0:T(8,128)} %get-tuple-element.6.factor_ref, f32[256,256]{1,0:T(8,128)} %get-tuple-element.7.invt_ref, f32[256,512]{1,0:T(8,128)} %get-tuple-element.8.cross_ref, bf16[4096,256]{1,0:T(8,128)(2,1)} %panel_hbm.3, ...), custom_call_target="tpu_custom_call" | custom-call | tf_op jit(solution)/shard_map/finish/pallas_call | solution.py:322

commit v4 on v3

--- a/solution.py
+++ b/solution.py
@@ -14,7 +14,7 @@
     return lax.dot_general(a, b, (((ca,), (cb,)), ((), ())), precision=HI, preferred_element_type=jnp.float32)
 
 
-def eliminate(block, r_ref, w_ref):
+def eliminate(block, r_ref, w_ref, midway):
     n = block.shape[0]
     groups = n // 8
     lane = lax.broadcasted_iota(jnp.int32, (8, n), 1)
@@ -45,13 +45,15 @@
         w = [w[t] - u[8 * t : 8 * t + 8, n:] for t in range(1, groups)] + [zero]
         return tuple(a), tuple(w)
 
-    lax.fori_loop(0, groups, group, (tuple(a), tuple(w)))
+    carry = lax.fori_loop(0, groups // 2, group, (tuple(a), tuple(w)))
+    midway()
+    lax.fori_loop(groups // 2, groups, group, carry)
 
 
 def fused_kernel(
-    n, ncol, scale, panel_hbm, slab_hbm, factor_ref, invt_ref, full_ref,
-    panel_ref, slab_ref, panel_sem, slab_sem, gram_ref, cross_ref, gbuf, cbuf, gfull, cfull, gown, cown, r_ref, w_ref,
-    gs_send, gs_recv, ga_send, ga_recv, fw_send, fw_recv, cs_send, cs_recv, ca_send, ca_recv,
+    n, ni, ncol, scale, panel_hbm, slab_hbm, factor_ref, invt_ref, full_ref,
+    panel_ref, slab_ref, panel_sem, slab_sem, gram_ref, cross_ref, gbuf, cbuf, partial, outer_buf, gfull, cfull, gown, cown, r_ref, w_ref,
+    gs_send, gs_recv, ga_send, ga_recv, fw_send, fw_recv, c1_send, c1_recv, c2_send, c2_recv, ca_send, ca_recv, cf_send, cf_recv,
 ):
     me, mc = lax.axis_index("row"), lax.axis_index("col")
     get_panel = pltpu.make_async_copy(panel_hbm, panel_ref, panel_sem)
@@ -61,7 +63,30 @@
     order = gram_ref.shape[1]
     part = gram_ref.shape[0]
     gchunk, cchunk = gown.shape[0], cown.shape[0]
-    gowners, cowners = part // gchunk, order // cchunk
+    gowners, cowners = part // gchunk, order // ni // cchunk
+    no = n // ni
+    mo, mi = me // ni, lax.rem(me, ni)
+
+    def outer(body):
+        def step(k, _):
+            body(lax.rem(mo + k, no))
+            return 0
+
+        lax.fori_loop(1, no, step, 0)
+
+    def inner(body):
+        def step(k, _):
+            body(lax.rem(mi + k, ni))
+            return 0
+
+        lax.fori_loop(1, ni, step, 0)
+
+    def pieces(body):
+        def step(k, _):
+            body(lax.rem(mo + 1 + k, cowners))
+            return 0
+
+        lax.fori_loop(0, cowners, step, 0)
 
     def peers(body):
         def step(k, _):
@@ -139,11 +164,20 @@
             fw_send.at[owner, dst], fw_recv.at[owner, col], me, dst,
         )
 
-    def cs(src, dst):
-        return remote(cross_ref.at[rows(dst, cchunk)], cbuf.at[src], cs_send.at[dst], cs_recv.at[src], dst, mc)
+    def piece(i, o):
+        return rows(i * cowners + o, cchunk)
+
+    def c1(src, dst, o):
+        return remote(cross_ref.at[piece(dst, o)], cbuf.at[src, o], c1_send.at[dst, o], c1_recv.at[src, o], mo * ni + dst, mc)
+
+    def c2(src, dst):
+        return remote(partial.at[dst], outer_buf.at[src], c2_send.at[dst], c2_recv.at[src], dst * ni + mi, mc)
 
     def ca(owner, dst):
-        return remote(cown, cfull.at[rows(owner, cchunk)], ca_send.at[dst], ca_recv.at[owner], dst, mc)
+        return remote(cown, cfull.at[piece(mi, owner)], ca_send.at[dst], ca_recv.at[owner], dst * ni + mi, mc)
+
+    def cf(src, dst, o, ref):
+        return remote(ref, cfull.at[piece(src, o)], cf_send.at[dst, o], cf_recv.at[src, o], mo * ni + dst, mc)
 
     peers(lambda p: owned(gowners, p, lambda: gs(me, p).start()))
 
@@ -172,7 +206,7 @@
             gown, gfull.at[grows(me, mc)], fw_send.at[me, q], fw_recv.at[me, mc], me, q).start())
 
     owned(gowners, me, sum_gram)
-    peers(lambda p: owned(cowners, p, lambda: cs(me, p).start()))
+    pieces(lambda o: inner(lambda i: c1(mi, i, o).start()))
 
     def relay(p):
         def go():
@@ -193,7 +227,36 @@
     cols(relayed)
 
     h = order // 2
-    eliminate(gfull[:h, :h], r_ref, w_ref)
+    def sum_inner():
+        def one(o):
+            partial[o] = cross_ref[piece(mi, o), :]
+
+            def add(i):
+                c1(i, mi, o).wait_recv()
+                partial[o] += cbuf[i, o]
+
+            inner(add)
+            pl.when(o != mo)(lambda: c2(mo, o).start())
+
+        pieces(one)
+
+    def relay_inner():
+        def one(o):
+            def go():
+                ca(o, mo).wait_recv()
+                inner(lambda i: cf(mi, i, o, cfull.at[piece(mi, o)]).start())
+
+            owned_outer(o, go)
+
+        outer(one)
+
+    def owned_outer(o, body):
+        if cowners == no:
+            body()
+        else:
+            pl.when(o < cowners)(body)
+
+    eliminate(gfull[:h, :h], r_ref, w_ref, sum_inner)
     w1 = w_ref[...]
     factor_ref[:h, :h] = r_ref[...]
     invt_ref[:h, :h] = w1
@@ -203,31 +266,34 @@
     invt_ref[:h, h:] = jnp.zeros((h, h), jnp.float32)
     lower = gfull[h:, h:] - mm(r12, r12, 0, 0)
 
-    def sum_cross():
-        cown[...] = cross_ref[rows(me, cchunk), :]
-
-        def add(p):
-            cs(p, me).wait_recv()
-            cown[...] += cbuf[p]
-
-        sources(add)
-        cfull[rows(me, cchunk), :] = cown[...]
-        peers(lambda p: ca(me, p).start())
-
-    owned(cowners, me, sum_cross)
-
-    eliminate(lower, r_ref, w_ref)
+    def sum_outer():
+        cown[...] = partial[mo]
+
+        def add(o):
+            c2(o, mo).wait_recv()
+            cown[...] += outer_buf[o]
+
+        outer(add)
+        cfull[piece(mi, mo), :] = cown[...]
+        outer(lambda o: ca(mo, o).start())
+        inner(lambda i: cf(mi, i, mo, cown).start())
+
+    owned_outer(mo, sum_outer)
+
+    eliminate(lower, r_ref, w_ref, relay_inner)
     w2 = w_ref[...]
     factor_ref[h:, h:] = r_ref[...]
     invt_ref[h:, h:] = w2
     invt_ref[h:, :h] = -mm(w2, mm(r12, w1, 0, 0))
 
-    peers(lambda p: owned(cowners, p, lambda: ca(p, me).wait_recv()))
+    pieces(lambda o: inner(lambda i: cf(i, mi, o, cown).wait_recv()))
     full_ref[...] = cfull[...]
     peers(lambda p: owned(gowners, p, lambda: gs(me, p).wait_send()))
-    peers(lambda p: owned(cowners, p, lambda: cs(me, p).wait_send()))
+    pieces(lambda o: inner(lambda i: c1(mi, i, o).wait_send()))
+    pieces(lambda o: pl.when(o != mo)(lambda: c2(mo, o).wait_send()))
+    pieces(lambda o: inner(lambda i: cf(mi, i, o, cown).wait_send()))
     owned(gowners, me, lambda: peers(lambda p: ga(me, p).wait_send()))
-    owned(cowners, me, lambda: peers(lambda p: ca(me, p).wait_send()))
+    owned_outer(mo, lambda: outer(lambda o: ca(mo, o).wait_send()))
 
     def sent(q):
         def each(o, _):
@@ -245,13 +311,18 @@
     part = order // ncol
     scale = 1.0 / (height * n)
     gchunk = max(8, part // n)
-    cchunk = max(8, order // n)
+    ni = 1
+    while 4 * ni * ni <= n and n % (2 * ni) == 0:
+        ni *= 2
+    no = n // ni
+    cowners = min(no, order // ni // 8)
+    cchunk = order // ni // cowners
     f32 = jnp.float32
     dma = pltpu.SemaphoreType.DMA
     square = jax.ShapeDtypeStruct((order, order), f32)
     h = order // 2
     return pl.pallas_call(
-        functools.partial(fused_kernel, n, ncol, scale),
+        functools.partial(fused_kernel, n, ni, ncol, scale),
         out_shape=(square, square, jax.ShapeDtypeStruct((order, width), f32)),
         in_specs=[pl.BlockSpec(memory_space=pl.ANY)] * 2,
         out_specs=[pl.BlockSpec(memory_space=pltpu.VMEM)] * 3,
@@ -262,7 +333,9 @@
             pltpu.VMEM((part, order), f32),
             pltpu.VMEM((order, width), f32),
             pltpu.VMEM((n, gchunk, order), f32),
-            pltpu.VMEM((n, cchunk, width), f32),
+            pltpu.VMEM((ni, cowners, cchunk, width), f32),
+            pltpu.VMEM((cowners, cchunk, width), f32),
+            pltpu.VMEM((no, cchunk, width), f32),
             pltpu.VMEM((order, order), f32),
             pltpu.VMEM((order, width), f32),
             pltpu.VMEM((gchunk, order), f32),
@@ -271,7 +344,8 @@
             pltpu.VMEM((h, h), f32),
             dma((n,)), dma((n,)), dma((n,)), dma((n,)),
             dma((n, ncol)), dma((n, ncol)),
-            dma((n,)), dma((n,)), dma((n,)), dma((n,)),
+            dma((ni, cowners)), dma((ni, cowners)), dma((no,)), dma((no,)),
+            dma((no,)), dma((no,)), dma((ni, cowners)), dma((ni, cowners)),
         ],
         compiler_params=pltpu.CompilerParams(collective_id=0, has_side_effects=True),
         name="sums_and_factor",

time: 53.1 us -> 49.8 us (0.938)
  the two profiles are of different devices: /device:TPU:29 before, /device:TPU:0 now
where the time goes in v4:
time: 49.8 us; the launch traced here: 49.6 us
  Pallas kernels  49 us (98%)
  between operations  0.64 us (1%)
    pallas_call x1, Pallas kernels, sums_and_factor(): pl.pallas_call(functools.partial(fused_kernel, n, ni, ncol, scale), out_s...  41.9 us
    pallas_call x1, Pallas kernels, finish(): pl.pallas_call(functools.partial(finish_kernel, tiles), out_shape=(jax.Sh...  7.07 us

profile of v4, /device:TPU:0, one launch (start us, length us, event | category | flops | bytes accessed | tf_op | source)
XLA Modules:
  0.0 49.6 jit_solution(16985057103896390137)
XLA Ops:
  0.6 41.9 %sums_and_factor.1 = (f32[256,256]{1,0:T(8,128)}, f32[256,256]{1,0:T(8,128)}, f32[256,512]{1,0:T(8,128)}) custom-call(bf16[4096,256]{1,0:T(8,128)(2,1)} %panel_hbm.3, bf16[4096,512]{1,0:T(8,128)(2,1)} %slab_hbm.3), custom_call_target="tpu_custom_call" | custom-call | tf_op jit(solution)/shard_map/sums_and_factor/pallas_call | solution.py:324
  42.6 7.1 %finish.1 = (f32[256,128]{1,0:T(8,128)}, f32[256,512]{1,0:T(8,128)}, bf16[4096,512]{1,0:T(8,128)(2,1)}) custom-call(f32[256,256]{1,0:T(8,128)} %get-tuple-element.6.factor_ref, f32[256,256]{1,0:T(8,128)} %get-tuple-element.7.invt_ref, f32[256,512]{1,0:T(8,128)} %get-tuple-element.8.cross_ref, bf16[4096,256]{1,0:T(8,128)(2,1)} %panel_hbm.3, ...), custom_call_target="tpu_custom_call" | custom-call | tf_op jit(solution)/shard_map/finish/pallas_call | solution.py:396

commit v5 on v4

--- a/solution.py
+++ b/solution.py
@@ -12,6 +12,12 @@
 
 def mm(a, b, ca=1, cb=0):
     return lax.dot_general(a, b, (((ca,), (cb,)), ((), ())), precision=HI, preferred_element_type=jnp.float32)
+
+
+def split(x):
+    high = x.astype(jnp.bfloat16).astype(jnp.float32)
+    mid = (x - high).astype(jnp.bfloat16).astype(jnp.float32)
+    return high, mid, x - high - mid
 
 
 def eliminate(block, r_ref, w_ref, midway):
@@ -39,7 +45,10 @@
         start = pl.multiple_of(8 * g, 8)
         r_ref[pl.ds(start, 8), :] = jnp.where(lane >= sub + 8 * g, pltpu.roll(top, 8 * g, 1), 0.0)
         w_ref[pl.ds(start, 8), :] = wtop
-        u = mm(top, jnp.concatenate([top, wtop], axis=1), 0, 0)
+        high, mid, low = split(jnp.concatenate([top, wtop], axis=1))
+        left = jnp.concatenate([x[:, :n] for x in (high, high, mid, mid, high, low)], axis=0).astype(jnp.bfloat16)
+        right = jnp.concatenate([high, mid, high, mid, low, high], axis=0).astype(jnp.bfloat16)
+        u = lax.dot_general(left, right, (((0,), (0,)), ((), ())), preferred_element_type=jnp.float32)
         zero = jnp.zeros((8, n), jnp.float32)
         a = [pltpu.roll(a[t] - u[8 * t : 8 * t + 8, :n], n - 8, 1) for t in range(1, groups)] + [zero]
         w = [w[t] - u[8 * t : 8 * t + 8, n:] for t in range(1, groups)] + [zero]

time: 49.8 us -> 48 us (0.964)
  Pallas kernels: 49 us -> 47.2 us
    pallas_call x1, Pallas kernels: 41.9 us -> 40.1 us  [sums_and_factor(): pl.pallas_call(functools.partial(fused_kernel, n, ni, ncol, scale), out_s...]
where the time goes in v5:
time: 48 us; the launch traced here: 47.8 us
  Pallas kernels  47.2 us (98%)
  between operations  0.64 us (1%)
    pallas_call x1, Pallas kernels, sums_and_factor(): pl.pallas_call(functools.partial(fused_kernel, n, ni, ncol, scale), out_s...  40.1 us
    pallas_call x1, Pallas kernels, finish(): pl.pallas_call(functools.partial(finish_kernel, tiles), out_shape=(jax.Sh...  7.08 us

profile of v5, /device:TPU:0, one launch (start us, length us, event | category | flops | bytes accessed | tf_op | source)
XLA Modules:
  0.0 47.8 jit_solution(3701933579023762285)
XLA Ops:
  0.6 40.1 %sums_and_factor.1 = (f32[256,256]{1,0:T(8,128)}, f32[256,256]{1,0:T(8,128)}, f32[256,512]{1,0:T(8,128)}) custom-call(bf16[4096,256]{1,0:T(8,128)(2,1)} %panel_hbm.3, bf16[4096,512]{1,0:T(8,128)(2,1)} %slab_hbm.3), custom_call_target="tpu_custom_call" | custom-call | tf_op jit(solution)/shard_map/sums_and_factor/pallas_call | solution.py:333
  40.7 7.1 %finish.1 = (f32[256,128]{1,0:T(8,128)}, f32[256,512]{1,0:T(8,128)}, bf16[4096,512]{1,0:T(8,128)(2,1)}) custom-call(f32[256,256]{1,0:T(8,128)} %get-tuple-element.6.factor_ref, f32[256,256]{1,0:T(8,128)} %get-tuple-element.7.invt_ref, f32[256,512]{1,0:T(8,128)} %get-tuple-element.8.cross_ref, bf16[4096,256]{1,0:T(8,128)(2,1)} %panel_hbm.3, ...), custom_call_target="tpu_custom_call" | custom-call | tf_op jit(solution)/shard_map/finish/pallas_call | solution.py:405
